TPU v7x, 256 devices: a whole 4x4x8 slice. The times are simulated.
256 devices in a mesh: dp: 32 (over x, z), feat: 8 (over y, core).
Axes of the slice: x: 4, y: 4, z: 8, core: 2. Of those that a mesh axis runs over, the one named last changes fastest.
Arguments:
- hidden_first: bfloat16 [2048, 4096], P('dp', 'feat'), may hold values from -6 to 6
- hidden_second: bfloat16 [2048, 4096], P('dp', 'feat'), may hold values from -11 to 11
- weight: bfloat16 [4096, 8192], P('dp', 'feat'), may hold values from -0.09375 to 0.09375
Outputs:
- total_loss: float32 [], replicated
- grad_weight: bfloat16 [4096, 8192], P('dp', 'feat')
- grad_first: bfloat16 [2048, 4096], P('dp', 'feat')
- grad_second: bfloat16 [2048, 4096], P('dp', 'feat')
All inputs are finite; a program needn't handle non-finite values.
Results may differ from a plain program's by a relative error of at most 0.015.
Values may be sent and summed in bfloat16 or wider, within the bound.
No kernel may reach another device: no remote copies, remote signals or barrier semaphores. Data moves between devices by JAX's collectives and lax.ppermute only.
A program may use at most 64 MiB of HBM per device.

v0:
```python
import jax
import jax.numpy as jnp
from jax import lax
from jax.sharding import PartitionSpec as P


def on_device(hidden_first, hidden_second, weight):
    dp_size = lax.axis_size("dp")
    feat_size = lax.axis_size("feat")
    row_count = hidden_first.shape[0]
    col_count = weight.shape[1]
    total_rows = row_count * dp_size * 1.0
    full_width = col_count * feat_size * 1.0
    full_first, full_second = (
        lax.all_gather(hidden_first, "feat", axis=1, tiled=True),
        lax.all_gather(hidden_second, "feat", axis=1, tiled=True),
    )
    stacked = jnp.concatenate([full_first, full_second], axis=0)
    whole_weight = lax.all_gather(weight, "dp", axis=0, tiled=True)
    outputs = jnp.dot(stacked, whole_weight, preferred_element_type=jnp.float32)
    views = outputs.reshape(2, row_count, col_count)
    col_sum = lax.psum(jnp.sum(views, axis=1), "dp")
    col_mean = col_sum / total_rows
    centered = views - col_mean[:, None, :]
    second_sum = lax.psum(jnp.sum(centered * centered, axis=1), "dp")
    variance = second_sum / (total_rows - 1.0)
    deviation = jnp.sqrt(variance + 0.0001)
    centered_half = centered.astype(jnp.bfloat16)
    gathered = lax.all_gather(centered_half, "dp", axis=1, tiled=True)
    gram_part = jnp.einsum(
        "vrc,vnc->vrn", centered_half, gathered, preferred_element_type=jnp.float32
    )
    gram_rows = lax.psum(gram_part.astype(jnp.bfloat16), "feat").astype(jnp.float32)
    gram_half = gram_rows.astype(jnp.bfloat16)
    spread = jnp.einsum("vrn,vnc->vrc", gram_half, gathered, preferred_element_type=jnp.float32)
    difference = views[0] - views[1]
    local_share = (
        25.0 * jnp.sum(difference * difference) / (total_rows * full_width)
        + 25.0 * jnp.sum(jax.nn.relu(1.0 - deviation)) / (full_width * dp_size)
        + (
            jnp.sum(gram_rows * gram_rows) / ((total_rows - 1.0) ** 2 * feat_size)
            - jnp.sum(variance * variance) / dp_size
        )
        / full_width
    )
    total_loss = lax.psum(local_share, ("dp", "feat"))
    inv_grad = 50.0 / 256.0 * jnp.stack([difference, -difference])
    binding = (deviation < 1.0).astype(jnp.float32)
    hinge_grad = (
        -(25.0 * total_rows / (256.0 * (total_rows - 1.0)))
        * (binding / deviation)[:, None, :]
        * centered
    )
    cov_grad = (
        4.0
        * total_rows
        / 256.0
        * (spread / (total_rows - 1.0) ** 2 - variance[:, None, :] * centered / (total_rows - 1.0))
    )
    grad_views = (inv_grad + hinge_grad + cov_grad).astype(jnp.bfloat16)
    flat_grads = grad_views.reshape(2 * row_count, col_count)
    input_terms = lax.dot_general(
        flat_grads, whole_weight, (((1,), (1,)), ((), ())), preferred_element_type=jnp.float32
    )
    input_grads = lax.psum_scatter(
        input_terms.astype(jnp.bfloat16), "feat", scatter_dimension=1, tiled=True
    )
    grad_first = input_grads[:row_count]
    grad_second = input_grads[row_count:]
    grad_weight = lax.psum_scatter(
        lax.dot_general(
            stacked, flat_grads, (((0,), (0,)), ((), ())), preferred_element_type=jnp.float32
        ).astype(jnp.bfloat16),
        "dp",
        scatter_dimension=0,
        tiled=True,
    )
    return (total_loss, grad_weight, grad_first, grad_second)


def solution(mesh):
    placed = (P("dp", "feat"), P("dp", "feat"), P("dp", "feat"))
    return jax.shard_map(
        on_device,
        mesh=mesh,
        in_specs=placed,
        out_specs=(P(), P("dp", "feat"), P("dp", "feat"), P("dp", "feat")),
        check_vma=False,
    )
```

profile of v0, /device:TPU:8, one launch (start us, length us, event | category | flops | bytes accessed | tf_op | source)
XLA Modules:
  0.0 638.5 jit_solution(8527642386405286671)
XLA Ops:
  7.2 0.7 all-gather.3.cloned.1.call-update
  7.9 0.0 all-gather.5.cloned.1.call-start
  7.9 13.5 %all_gather.12 = bf16[64,4096]{1,0:T(8,128)(2,1)S(1)} all-gather(bf16[64,512]{1,0:T(8,128)(2,1)} %param.3), channel_id=1, replica_groups=mesh['dp'=32,'feat'=8] {'feat'}, dimensions={1}, use_global_device_ids=true | all-gather | bytes 589824 | tf_op jit(solution)/shard_map/all_gather | solution.py:15
  21.5 13.3 %all_gather.13 = bf16[64,4096]{1,0:T(8,128)(2,1)S(1)} all-gather(bf16[64,512]{1,0:T(8,128)(2,1)} %param.4), channel_id=1, replica_groups=mesh['dp'=32,'feat'=8] {'feat'}, dimensions={1}, use_global_device_ids=true | all-gather | bytes 589824 | tf_op jit(solution)/shard_map/all_gather | solution.py:16
  34.9 76.4 %all-gather.3.cloned.1.call-done = bf16[4096,1024]{1,0:T(8,128)(2,1)} async-done(((bf16[128,1024]{1,0:T(8,128)(2,1)}), bf16[4096,1024]{1,0:T(8,128)(2,1)}) %all-gather.3.cloned.1.call-update) | async-done | bytes 8388624 | tf_op jit(solution)/shard_map/all_gather | solution.py:19
  111.3 4.7 bitcast_reduce_fusion
  115.9 72.4 %psum.28 = f32[2,1024]{1,0:T(2,128)S(1)} all-reduce(f32[2,1024]{1,0:T(2,128)S(1)} %get-tuple-element.15), channel_id=1, replica_groups=mesh['dp'=32,'feat'=8] {'dp'}, use_global_device_ids=true, to_apply=%region_2.0 | all-reduce | flops 2048 | bytes 16384 | tf_op jit(solution)/shard_map/psum | solution.py:22
  188.3 0.8 fusion.5
  189.1 0.0 all-reduce.2.cloned.1.call-start
  189.2 72.3 %psum.29 = f32[2,1024]{1,0:T(2,128)S(1)} all-reduce(f32[2,1024]{1,0:T(2,128)S(1)} %get-tuple-element.7), channel_id=1, replica_groups=mesh['dp'=32,'feat'=8] {'dp'}, use_global_device_ids=true, to_apply=%region_4.0 | all-reduce | flops 2048 | bytes 16384 | tf_op jit(solution)/shard_map/psum | solution.py:25
  261.4 19.3 %all-gather.5.cloned.1.call-done = bf16[2,2048,1024]{2,1,0:T(8,128)(2,1)} async-done(((bf16[2,64,1024]{2,1,0:T(8,128)(2,1)}), bf16[2,2048,1024]{2,1,0:T(8,128)(2,1)}) %all-gather.5.cloned.1.call-update) | async-done | bytes 8388624 | tf_op jit(solution)/shard_map/all_gather | solution.py:29
  280.8 6.9 %convolution_convert_fusion.2 = bf16[2,64,2048]{2,1,0:T(8,128)(2,1)} fusion(bf16[2,64,1024]{2,1,0:T(8,128)(2,1)} %get-tuple-element.6, bf16[2,2048,1024]{2,1,0:T(8,128)(2,1)} %all-gather.5.cloned.1.call-done), kind=kOutput, calls=%fused_computation.2 | convolution fusion | flops 537133056 | bytes 9175040 | tf_op jit(solution)/shard_map/vrc,vnc->vrn/dot_general | solution.py:30
  287.8 0.0 reduce-scatter.5.cloned.1.call-start
  287.8 0.6 multiply_reduce_fusion.3
  288.4 0.7 fusion.8
  289.1 59.9 %all-reduce.2.cloned.1.call-done = bf16[2,64,2048]{2,1,0:T(8,128)(2,1)} async-done(((bf16[2,64,2048]{2,1,0:T(8,128)(2,1)}), bf16[2,64,2048]{2,1,0:T(8,128)(2,1)}) %all-reduce.2.cloned.1.call-update) | async-done | bytes 524304 | tf_op jit(solution)/shard_map/psum | solution.py:33
  349.0 5.3 fusion.3
  354.3 7.3 %convolution_convert_fusion.1 = bf16[128,4096]{1,0:T(8,128)(2,1)} fusion(bf16[128,1024]{1,0:T(8,128)(2,1)S(1)} %bitcast.24, bf16[4096,1024]{1,0:T(8,128)(2,1)} %all-gather.3.cloned.1.call-done), kind=kOutput, calls=%fused_computation.1 | convolution fusion | flops 1074266112 | bytes 9699328 | tf_op jit(solution)/shard_map/dot_general | solution.py:62
  361.7 0.0 reduce-scatter.3.cloned.1.call-start
  361.7 5.6 convolution_convert_fusion
  369.3 0.9 multiply_reduce_fusion
  370.8 77.3 %psum.31 = f32[]{:T(128)} all-reduce(f32[]{:T(128)S(6)} %add.33), channel_id=1, replica_groups=mesh['dp'=32,'feat'=8] {'dp','feat'}, use_global_device_ids=true, to_apply=%region_9.10 | all-reduce | flops 1 | bytes 8 | tf_op jit(solution)/shard_map/psum | solution.py:46
  448.2 1.5 fusion.9
  449.7 182.3 %reduce-scatter.3.cloned.1.call-done = bf16[128,1024]{1,0:T(8,128)(2,1)} async-done(((bf16[4096,1024]{1,0:T(8,128)(2,1)}), bf16[128,1024]{1,0:T(8,128)(2,1)}) %reduce-scatter.3.cloned.1.call-update) | async-done | bytes 262160 | tf_op jit(solution)/shard_map/reduce_scatter | solution.py:70
  (11 shorter events, 0.2 us)
Async XLA Ops:
  7.2 104.1 %all-gather.3.cloned.1.call-start = ((), (), s32[]{:S(2)}) async-start(), calls=%async_computation.2 | async-start | bytes 8650752 | tf_op jit(solution)/shard_map/all_gather | solution.py:19
  7.9 272.9 %all-gather.5.cloned.1.call-start = ((), (), s32[]{:S(2)}) async-start(), calls=%async_computation.3 | async-start | bytes 8650752 | tf_op jit(solution)/shard_map/all_gather | solution.py:29
  189.1 159.9 %all-reduce.2.cloned.1.call-start = ((), (), s32[]{:S(2)}) async-start(), calls=%async_computation.4 | async-start | bytes 1048576 | tf_op jit(solution)/shard_map/psum | solution.py:33
  287.8 160.4 %reduce-scatter.5.cloned.1.call-start = ((), (), s32[]{:S(2)}) async-start(), calls=%async_computation.6 | async-start | bytes 1179648 | tf_op jit(solution)/shard_map/reduce_scatter | solution.py:65
  361.7 7.6 %copy-start = (bf16[2,64,2048]{2,1,0:T(8,128)(2,1)S(1)}, bf16[2,64,2048]{2,1,0:T(8,128)(2,1)}, u32[]{:S(2)}) copy-start(bf16[2,64,2048]{2,1,0:T(8,128)(2,1)} %all-reduce.2.cloned.1.call-done) | copy-start | bytes 1572868
  361.7 270.3 %reduce-scatter.3.cloned.1.call-start = ((), (), s32[]{:S(2)}) async-start(), calls=%async_computation.5 | async-start | bytes 8650752 | tf_op jit(solution)/shard_map/reduce_scatter | solution.py:70
Sparse Core Ops, SparseCore 0:
  10.6 100.6 all-gather.2
  189.2 91.5 all-gather.4
  287.9 61.1 all-reduce.1
  361.8 33.2 reduce-scatter.4
  399.5 232.4 reduce-scatter.2
where the time goes:
time: 639 us
  waiting for transfers between devices  339 us (53%)
  blocking collectives  249 us (39%)
  matrix products  29.8 us (5%)
  between operations  16.5 us (3%)
    reduce_scatter x1, waiting for transfers between devices, on_device(): lax.psum_scatter(lax.dot_general(stacked, flat_grads, (((0,), (0,)), ((),...  182 us
    psum x1, blocking collectives, on_device(): total_loss = lax.psum(local_share, ('dp', 'feat'))  77.3 us
    all_gather x1, waiting for transfers between devices, on_device(): whole_weight = lax.all_gather(weight, 'dp', axis=0, tiled=True)  76.4 us
    psum x1, blocking collectives, on_device(): col_sum = lax.psum(jnp.sum(views, axis=1), 'dp')  72.4 us
    psum x1, blocking collectives, on_device(): second_sum = lax.psum(jnp.sum(centered * centered, axis=1), 'dp')  72.3 us
    psum x1, waiting for transfers between devices, on_device(): lax.psum(gram_part.astype(jnp.bfloat16), 'feat').astype(jnp.float32)  59.9 us
    all_gather x1, waiting for transfers between devices, on_device(): gathered = lax.all_gather(centered_half, 'dp', axis=1, tiled=True)  19.3 us
    all_gather x1, blocking collectives, on_device(): lax.all_gather(hidden_first, 'feat', axis=1, tiled=True)  13.5 us
  transfers between devices with their start and end apart: 5, of which 4 were waited for; matrix products, arithmetic and copies ran while one was open for 1% of the time, Pallas kernels for 0%

commit v1 on v0

v1 whole, which is shorter than its diff:
```python
import jax
import jax.numpy as jnp
from jax import lax
from jax.sharding import Mesh, PartitionSpec as P

BF = jnp.bfloat16
F32 = jnp.float32
NX, NZ, NY, NC = 4, 8, 4, 2
FEAT = ("y", "c")
CHIPS = ("x", "y")


def swap_xy(v):
    pairs = [(a * NY + b, b * NX + a) for a in range(NX) for b in range(NY)]
    return lax.ppermute(v, ("x", "y"), pairs)


def swap_core(v):
    return lax.ppermute(v, "c", [(0, 1), (1, 0)])


def split3(v):
    hi = v.astype(BF)
    rest = v - hi.astype(F32)
    mid = rest.astype(BF)
    low = (rest - mid.astype(F32)).astype(BF)
    return hi, mid, low


def dot(a, b, ca, cb):
    return lax.dot_general(a, b, (((ca,), (cb,)), ((), ())), preferred_element_type=F32)


def on_device(hidden_first, hidden_second, weight):
    core = lax.axis_index("c")
    rows, kpart = hidden_first.shape
    cols = weight.shape[1]
    total_rows = rows * NX * NZ * 1.0
    full_width = cols * NY * NC * 1.0
    blk = rows * NX
    kq = kpart * NC
    sub = cols // NX

    wq = lax.all_gather(weight, "z", axis=0, tiled=True)
    moved = swap_xy(jnp.stack([hidden_first, hidden_second]))

    def whole_quarter(v):
        got = lax.all_gather(v, FEAT, axis=0, tiled=False)
        got = got.reshape(NY, NC, rows, kpart)
        return jnp.transpose(got, (0, 2, 1, 3)).reshape(blk, kq)

    hq = jnp.concatenate([whole_quarter(moved[0]), whole_quarter(moved[1])], axis=0)

    row_sum = lax.psum(jnp.sum(hq.reshape(2, blk, kq).astype(F32), axis=1), "z")
    mean_in = row_sum / total_rows
    mean_rows = jnp.concatenate(split3(mean_in), axis=0)
    mean_terms = dot(mean_rows, wq, 1, 0)
    mean_part = mean_terms[0:2] + mean_terms[2:4] + mean_terms[4:6]

    part = dot(hq, wq, 1, 0).reshape(2, blk, cols) - mean_part[:, None, :]
    part = part.astype(BF).reshape(2 * blk, NX, sub)
    part = jnp.transpose(part, (1, 0, 2))
    parts = lax.all_to_all(part, "x", split_axis=0, concat_axis=0, tiled=True)
    centered = jnp.sum(parts.astype(F32), axis=0).reshape(2, blk, sub)

    half = centered.astype(BF)
    mine = jnp.where(core == 0, half[0], half[1])
    theirs = jnp.where(core == 0, half[1], half[0])
    own_rows = jnp.concatenate([mine, swap_core(theirs)], axis=1)
    gathered = lax.all_gather(own_rows, "z", axis=0, tiled=True)

    mean_cols = lax.psum_scatter(
        mean_part.reshape(2, NX, sub).transpose(1, 0, 2), "x", scatter_dimension=0, tiled=True
    )[0]
    difference = centered[0] - centered[1] + (mean_cols[0] - mean_cols[1])[None, :]

    wide = gathered.astype(F32)
    var_view = jnp.sum(wide * wide, axis=0) / (total_rows - 1.0)
    dev_view = jnp.sqrt(var_view + 0.0001)
    var_own = var_view[:sub]
    var_back = swap_core(var_view[sub:].reshape(1, sub))[0]

    gram_part = dot(own_rows, gathered, 1, 1).astype(BF)
    pieces = lax.all_to_all(
        gram_part.reshape(NX * NY, blk // (NX * NY), -1), CHIPS, split_axis=0, concat_axis=0, tiled=True
    )
    gram_rows = jnp.sum(pieces.astype(F32), axis=0)
    gram_half = lax.all_gather(gram_rows.astype(BF), CHIPS, axis=0, tiled=True)
    spread_view = dot(gram_half, gathered, 1, 0)
    spread_own = spread_view[:, :sub]
    spread_back = swap_core(spread_view[:, sub:])

    first = core == 0
    spread = jnp.stack(
        [jnp.where(first, spread_own, spread_back), jnp.where(first, spread_back, spread_own)]
    )
    variance = jnp.stack([jnp.where(first, var_own, var_back), jnp.where(first, var_back, var_own)])
    deviation = jnp.sqrt(variance + 0.0001)

    inv_grad = 50.0 / 256.0 * jnp.stack([difference, -difference])
    binding = (deviation < 1.0).astype(F32)
    hinge_grad = (
        -(25.0 * total_rows / (256.0 * (total_rows - 1.0)))
        * (binding / deviation)[:, None, :]
        * centered
    )
    cov_grad = (
        4.0
        * total_rows
        / 256.0
        * (spread / (total_rows - 1.0) ** 2 - variance[:, None, :] * centered / (total_rows - 1.0))
    )
    grad_views = (inv_grad + hinge_grad + cov_grad).astype(BF).reshape(2 * blk, sub)
    grads = lax.all_gather(grad_views, "x", axis=1, tiled=True)

    weight_part = dot(hq, grads, 0, 0).astype(BF)
    grad_weight = lax.psum_scatter(weight_part, "z", scatter_dimension=0, tiled=True)

    input_part = dot(grads, wq, 1, 1).astype(BF)
    input_part = input_part.reshape(2, NX, rows, NC, kpart).transpose(1, 3, 0, 2, 4)
    input_part = input_part.reshape(NX * NC, 2, rows, kpart)
    input_parts = lax.all_to_all(input_part, FEAT, split_axis=0, concat_axis=0, tiled=True)
    input_grads = swap_xy(jnp.sum(input_parts.astype(F32), axis=0).astype(BF))

    share = (
        25.0 * jnp.sum(difference * difference) / (total_rows * full_width)
        + 25.0 * jnp.sum(jax.nn.relu(1.0 - dev_view)) / (full_width * NZ)
        + (
            jnp.sum(gram_rows * gram_rows) / (total_rows - 1.0) ** 2
            - jnp.sum(var_view * var_view) / NZ
        )
        / full_width
    )
    total_loss = lax.psum(lax.psum(lax.psum(share, "x"), FEAT), "z")
    return (total_loss, grad_weight, input_grads[0], input_grads[1])


def solution(mesh):
    grid = Mesh(mesh.devices.reshape(NX, NZ, NY, NC), ("x", "z", "y", "c"))
    placed = P(("x", "z"), ("y", "c"))
    return jax.shard_map(
        on_device,
        mesh=grid,
        in_specs=(placed, placed, placed),
        out_specs=(P(), placed, placed, placed),
        check_vma=False,
    )
```

time: 639 us -> 325 us (0.51)
  waiting for transfers between devices: 339 us -> 117 us
  blocking collectives: 249 us -> 138 us
  matrix products: 29.8 us -> 16.2 us
  local copies, waits for them, and re-layouts: 1.61 us -> 14.3 us
  starting transfers between devices: 0.2 us -> 11 us
    reduce_scatter x2 -> x1, waiting for transfers between devices: 182 us -> 0.01 us  [on_device(): lax.psum_scatter(weight_part, 'z', scatter_dimension=0, tiled=True)]
    psum x3 -> x4, blocking collectives: 222 us -> 59.9 us  [the longest x3 39.6 us: on_device(): total_loss = lax.psum(lax.psum(lax.psum(share, 'x'), FEAT), 'z')]
    psum x1 -> x0, waiting for transfers between devices: 59.9 us -> none  [on_device(): lax.psum(gram_part.astype(jnp.bfloat16), 'feat').astype(jnp.float32)]
    all_to_all x0 -> x2, blocking collectives: none -> 38 us  [the longest x1 19.2 us: on_device(): lax.all_to_all(input_part, FEAT, split_axis=0, concat_axis=0, tiled=True)]
    dot_general x5 -> x6, matrix products: 29.8 us -> 16.2 us  [dot(): lax.dot_general(a, b, (((ca,), (cb,)), ((), ())), preferred_element_type=...]
    all_to_all x0 -> x1, waiting for transfers between devices: none -> 12 us  [on_device(): parts = lax.all_to_all(part, 'x', split_axis=0, concat_axis=0, tiled=True)]
    unnamed x0 -> x1, blocking collectives: none -> 8.92 us
    ppermute x0 -> x5, waiting for transfers between devices: none -> 7.55 us  [the longest x2 4.74 us: swap_xy(): return lax.ppermute(v, ('x', 'y'), pairs)]
  transfers between devices with their start and end apart: 5 -> 11, of which waited for: 4 -> 7; matrix products, arithmetic and copies ran while one was open for 1% -> 4% of each run, Pallas kernels for 0% -> 0%
where the time goes in v1:
time: 325 us; the launch traced here: 322 us
  blocking collectives  138 us (42%)
  waiting for transfers between devices  117 us (36%)
  between operations  16.7 us (5%)
  matrix products  16.2 us (5%)
  local copies, waits for them, and re-layouts  14.3 us (4%)
  starting transfers between devices  11 us (3%)
  other arithmetic  9.27 us (3%)
    psum x3, blocking collectives, on_device(): total_loss = lax.psum(lax.psum(lax.psum(share, 'x'), FEAT), 'z')  39.6 us
    all_gather x1, waiting for transfers between devices, on_device(): gathered = lax.all_gather(own_rows, 'z', axis=0, tiled=True)  36.8 us
    all_gather x1, waiting for transfers between devices, on_device(): gram_half = lax.all_gather(gram_rows.astype(BF), CHIPS, axis=0, tiled=True)  31.9 us
    all_gather x2, blocking collectives, whole_quarter(): got = lax.all_gather(v, FEAT, axis=0, tiled=False)  31.7 us
    all_gather x1, waiting for transfers between devices, on_device(): grads = lax.all_gather(grad_views, 'x', axis=1, tiled=True)  27.6 us
    psum x1, blocking collectives, on_device(): row_sum = lax.psum(jnp.sum(hq.reshape(2, blk, kq).astype(F32), axis=1), 'z')  20.3 us
    all_to_all x1, blocking collectives, on_device(): lax.all_to_all(input_part, FEAT, split_axis=0, concat_axis=0, tiled=True)  19.2 us
    all_to_all x1, blocking collectives, on_device(): lax.all_to_all(gram_part.reshape(NX * NY, blk // (NX * NY), -1), CHIPS, s...  18.7 us
  transfers between devices with their start and end apart: 11, of which 7 were waited for; matrix products, arithmetic and copies ran while one was open for 4% of the time, Pallas kernels for 0%

profile of v1, /device:TPU:8, one launch (start us, length us, event | category | flops | bytes accessed | tf_op | source)
XLA Modules:
  0.0 322.5 jit_solution(2281793145193502178)
XLA Ops:
  8.8 3.3 %collective-permute-start = (bf16[2,64,512]{2,1,0:T(8,128)(2,1)S(1)}, bf16[2,64,512]{2,1,0:T(8,128)(2,1)S(1)}, u32[]{:S(2)}, u32[]{:S(2)}) collective-permute-start(bf16[2,64,512]{2,1,0:T(8,128)(2,1)S(1)} %pad_maximum_fusion.1), channel_id=1, source_target_pairs={{0,0},{2,64},{4,128},{6,192},{64,2},{66,66},{68,130},{70,194},{128... | collective-permute-start | bytes 393224 | tf_op jit(solution)/shard_map/ppermute | solution.py:15
  12.1 4.7 %collective-permute-done = bf16[2,64,512]{2,1,0:T(8,128)(2,1)S(1)} collective-permute-done((bf16[2,64,512]{2,1,0:T(8,128)(2,1)S(1)}, bf16[2,64,512]{2,1,0:T(8,128)(2,1)S(1)}, u32[]{:S(2)}, u32[]{:S(2)}) %collective-permute-start) | collective-permute-done | bytes 131104 | tf_op jit(solution)/shard_map/ppermute | solution.py:15
  16.8 18.6 %all_gather.18 = bf16[8,64,512]{2,1,0:T(8,128)(2,1)S(1)} all-gather(bf16[1,64,512]{2,1,0:T(8,128)(2,1)S(1)} %get-tuple-element.17), channel_id=1, replica_groups=mesh['x'=4,'z'=8,'y'=4,'c'=2] {'y','c'}, dimensions={0}, use_global_device_ids=true | all-gather | bytes 589824 | tf_op jit(solution)/shard_map/all_gather | solution.py:48
  36.0 13.1 %all_gather.19 = bf16[8,64,512]{2,1,0:T(8,128)(2,1)S(1)} all-gather(bf16[1,64,512]{2,1,0:T(8,128)(2,1)S(1)} %get-tuple-element.16), channel_id=1, replica_groups=mesh['x'=4,'z'=8,'y'=4,'c'=2] {'y','c'}, dimensions={0}, use_global_device_ids=true | all-gather | bytes 589824 | tf_op jit(solution)/shard_map/all_gather | solution.py:48
  50.1 20.3 %psum.28 = f32[2,1024]{1,0:T(2,128)S(1)} all-reduce(f32[2,1024]{1,0:T(2,128)S(1)} %convert_reduce_fusion), channel_id=1, replica_groups=mesh['x'=4,'z'=8,'y'=4,'c'=2] {'z'}, use_global_device_ids=true, to_apply=%region_1.0 | all-reduce | flops 2048 | bytes 16384 | tf_op jit(solution)/shard_map/psum | solution.py:54
  72.6 2.5 fusion.21
  75.1 2.2 reshape.133
  78.9 3.2 sub.49
  82.1 2.1 fusion
  85.3 3.5 %all-to-all-start = ((bf16[4,512,256]{2,1,0:T(8,128)(2,1)}), bf16[4,512,256]{2,1,0:T(8,128)(2,1)S(1)}, u32[]{:S(2)}, u32[]{:S(2)}) async-start(bf16[4,512,256]{2,1,0:T(8,128)(2,1)} %copy.22), calls=%async_computation | async-start | bytes 2097152 | tf_op jit(solution)/shard_map/all_to_all | solution.py:63
  88.9 12.0 %all-to-all-done = bf16[4,512,256]{2,1,0:T(8,128)(2,1)S(1)} async-done(((bf16[4,512,256]{2,1,0:T(8,128)(2,1)}), bf16[4,512,256]{2,1,0:T(8,128)(2,1)S(1)}, u32[]{:S(2)}, u32[]{:S(2)}) %all-to-all-start) | async-done | bytes 1048608 | tf_op jit(solution)/shard_map/all_to_all | solution.py:63
  103.4 36.8 %all-gather.7.cloned.1.call-done = bf16[2048,512]{1,0:T(8,128)(2,1)} async-done(((bf16[256,512]{1,0:T(8,128)(2,1)}), bf16[2048,512]{1,0:T(8,128)(2,1)}) %all-gather.7.cloned.1.call-update) | async-done | bytes 2097168 | tf_op jit(solution)/shard_map/all_gather | solution.py:70
  140.2 2.3 convolution_convert_fusion
  142.5 18.7 %all_to_all.15 = bf16[16,16,2048]{2,1,0:T(8,128)(2,1)S(1)} all-to-all(bf16[16,16,2048]{2,1,0:T(8,128)(2,1)S(1)} %bitcast.73), channel_id=1, replica_groups=mesh['x'=4,'z'=8,'y'=4,'c'=2] {'x','y'}, dimensions={0} | all-to-all | bytes 2097152 | tf_op jit(solution)/shard_map/all_to_all | solution.py:84
  163.3 8.9 %all-reduce = f32[4,2,256]{2,1,0:T(2,128)S(1)} all-reduce(f32[4,2,256]{2,1,0:T(2,128)S(1)} %bitcast.82), channel_id=2, replica_groups=mesh['x'=4,'z'=8,'y'=4,'c'=2] {'x'}, use_global_device_ids=true, to_apply=%region_3.4.clone | all-reduce | flops 2048 | bytes 16384
  174.2 31.9 %all-gather.9.cloned.1.call-done = bf16[256,2048]{1,0:T(8,128)(2,1)} async-done(((bf16[16,2048]{1,0:T(8,128)(2,1)}), bf16[256,2048]{1,0:T(8,128)(2,1)}) %all-gather.9.cloned.1.call-update) | async-done | bytes 1048592 | tf_op jit(solution)/shard_map/all_gather | solution.py:88
  210.9 27.6 %all-gather.11.cloned.1.call-done = bf16[512,1024]{1,0:T(8,128)(2,1)} async-done(((bf16[512,256]{1,0:T(8,128)(2,1)}), bf16[512,1024]{1,0:T(8,128)(2,1)}) %all-gather.11.cloned.1.call-update) | async-done | bytes 1048592 | tf_op jit(solution)/shard_map/all_gather | solution.py:114
  238.5 3.8 %convolution_convert_fusion.1 = bf16[1024,1024]{1,0:T(8,128)(2,1)} fusion(bf16[512,1024]{1,0:T(8,128)(2,1)S(1)} %copy-done.2, bf16[512,1024]{1,0:T(8,128)(2,1)} %all-gather.11.cloned.1.call-done), kind=kOutput, calls=%fused_computation.6 | convolution fusion | flops 1074790400 | bytes 4194304 | tf_op jit(solution)/shard_map/dot_general | solution.py:31
  243.9 3.5 %convolution_convert_fusion.2 = bf16[512,1024]{1,0:T(8,128)(2,1)} fusion(bf16[512,1024]{1,0:T(8,128)(2,1)} %all-gather.11.cloned.1.call-done, bf16[1024,1024]{1,0:T(8,128)(2,1)S(1)} %copy-done.4), kind=kOutput, calls=%fused_computation.7 | convolution fusion | flops 1074266112 | bytes 4194304 | tf_op jit(solution)/shard_map/dot_general | solution.py:31
  249.5 19.2 %all_to_all.16 = bf16[8,2,64,512]{3,2,1,0:T(8,128)(2,1)S(1)} all-to-all(bf16[8,2,64,512]{3,2,1,0:T(8,128)(2,1)S(1)} %bitcast.74), channel_id=1, replica_groups=mesh['x'=4,'z'=8,'y'=4,'c'=2] {'y','c'}, dimensions={0} | all-to-all | bytes 2097152 | tf_op jit(solution)/shard_map/all_to_all | solution.py:122
  268.8 3.6 %collective-permute-start.4 = (bf16[2,64,512]{2,1,0:T(8,128)(2,1)S(1)}, bf16[2,64,512]{2,1,0:T(8,128)(2,1)S(1)}, u32[]{:S(2)}, u32[]{:S(2)}) collective-permute-start(bf16[2,64,512]{2,1,0:T(8,128)(2,1)S(1)} %reduce_sum.92), channel_id=1, source_target_pairs={{0,0},{2,64},{4,128},{6,192},{64,2},{66,66},{68,130},{70,194},{128... | collective-permute-start | bytes 393224 | tf_op jit(solution)/shard_map/ppermute | solution.py:15
  275.7 10.9 %psum.29 = f32[]{:T(128)} all-reduce(f32[]{:T(128)S(6)} %add.68), channel_id=1, replica_groups=mesh['x'=4,'z'=8,'y'=4,'c'=2] {'x'}, use_global_device_ids=true, to_apply=%region_10.11 | all-reduce | flops 1 | bytes 8 | tf_op jit(solution)/shard_map/psum | solution.py:134
  286.6 10.6 %psum.30 = f32[]{:T(128)} all-reduce(f32[]{:T(128)} %psum.29), channel_id=1, replica_groups=mesh['x'=4,'z'=8,'y'=4,'c'=2] {'y','c'}, use_global_device_ids=true, to_apply=%region_11.12 | all-reduce | flops 1 | bytes 8 | tf_op jit(solution)/shard_map/psum | solution.py:134
  297.2 18.1 %psum.31 = f32[]{:T(128)} all-reduce(f32[]{:T(128)} %psum.30), channel_id=1, replica_groups=mesh['x'=4,'z'=8,'y'=4,'c'=2] {'z'}, use_global_device_ids=true, to_apply=%region_12.13 | all-reduce | flops 1 | bytes 8 | tf_op jit(solution)/shard_map/psum | solution.py:134
  (69 shorter events, 24.3 us)
Async XLA Ops:
  7.2 63.2 %all-gather.5.cloned.1.call-start = ((), (), s32[]{:S(2)}) async-start(), calls=%async_computation.4 | async-start | bytes 2359296 | tf_op jit(solution)/shard_map/all_gather | solution.py:44
  8.8 8.0 %collective-permute-start = (bf16[2,64,512]{2,1,0:T(8,128)(2,1)S(1)}, bf16[2,64,512]{2,1,0:T(8,128)(2,1)S(1)}, u32[]{:S(2)}, u32[]{:S(2)}) collective-permute-start(bf16[2,64,512]{2,1,0:T(8,128)(2,1)S(1)} %pad_maximum_fusion.1), channel_id=1, source_target_pairs={{0,0},{2,64},{4,128},{6,192},{64,2},{66,66},{68,130},{70,194},{128... | collective-permute-start | bytes 393224 | tf_op jit(solution)/shard_map/ppermute | solution.py:15
  49.8 22.7 %copy-start.1 = (bf16[512,1024]{1,0:T(8,128)(2,1)}, bf16[512,1024]{1,0:T(8,128)(2,1)S(1)}, u32[]{:S(2)}) copy-start(bf16[512,1024]{1,0:T(8,128)(2,1)S(1)} %constant_dynamic-update-slice_fusion) | copy-start | bytes 3145732
  70.4 2.2 copy-start.3
  85.3 15.6 %all-to-all-start = ((bf16[4,512,256]{2,1,0:T(8,128)(2,1)}), bf16[4,512,256]{2,1,0:T(8,128)(2,1)S(1)}, u32[]{:S(2)}, u32[]{:S(2)}) async-start(bf16[4,512,256]{2,1,0:T(8,128)(2,1)} %copy.22), calls=%async_computation | async-start | bytes 2097152 | tf_op jit(solution)/shard_map/all_to_all | solution.py:63
  88.9 51.3 %all-gather.7.cloned.1.call-start = ((), (), s32[]{:S(2)}) async-start(), calls=%async_computation.5 | async-start | bytes 2359296 | tf_op jit(solution)/shard_map/all_gather | solution.py:70
  101.2 1.4 collective-permute-start.1
  103.4 102.7 %all-gather.9.cloned.1.call-start = ((), (), s32[]{:S(2)}) async-start(), calls=%async_computation.6 | async-start | bytes 1114112 | tf_op jit(solution)/shard_map/all_gather | solution.py:88
  142.5 20.3 %copy-start.5 = (u32[256]{0:T(256)S(1)}, u32[256]{0:T(256)}, u32[]{:S(2)}) copy-start(u32[256]{0:T(256)} %constant.54) | copy-start | bytes 3076
  142.5 30.5 %copy-start = (bf16[2048,512]{1,0:T(8,128)(2,1)S(1)}, bf16[2048,512]{1,0:T(8,128)(2,1)}, u32[]{:S(2)}) copy-start(bf16[2048,512]{1,0:T(8,128)(2,1)} %all-gather.7.cloned.1.call-done) | copy-start | bytes 6291460
  162.7 75.8 %all-gather.11.cloned.1.call-start = ((), (), s32[]{:S(2)}) async-start(), calls=%async_computation.7 | async-start | bytes 1310720 | tf_op jit(solution)/shard_map/all_gather | solution.py:114
  174.2 33.9 %collective-permute-start.2 = (f32[1,256]{1,0:T(1,128)S(1)}, f32[1,256]{1,0:T(1,128)S(1)}, u32[]{:S(2)}, u32[]{:S(2)}) collective-permute-start(f32[1,256]{1,0:T(1,128)S(1)} %bitcast.88), channel_id=1, source_target_pairs={{0,1},{1,0},{2,3},{3,2},{4,5},{5,4},{6,7},{7,6},{8,9},{9,8},{10,11... | collective-permute-start | bytes 3080 | tf_op jit(solution)/shard_map/ppermute | solution.py:19
  208.0 1.6 collective-permute-start.3
  209.7 28.8 %copy-start.2 = (bf16[512,1024]{1,0:T(8,128)(2,1)S(1)}, bf16[512,1024]{1,0:T(8,128)(2,1)}, u32[]{:S(2)}) copy-start(bf16[512,1024]{1,0:T(8,128)(2,1)} %copy-done.1) | copy-start | bytes 3145732
  210.7 105.3 %reduce-scatter.2.cloned.1.call-start = ((), (), s32[]{:S(2)}) async-start(), calls=%async_computation.8 | async-start | bytes 2359296 | tf_op jit(solution)/shard_map/reduce_scatter | solution.py:117
  242.3 1.6 copy-start.4
  268.8 46.4 %collective-permute-start.4 = (bf16[2,64,512]{2,1,0:T(8,128)(2,1)S(1)}, bf16[2,64,512]{2,1,0:T(8,128)(2,1)S(1)}, u32[]{:S(2)}, u32[]{:S(2)}) collective-permute-start(bf16[2,64,512]{2,1,0:T(8,128)(2,1)S(1)} %reduce_sum.92), channel_id=1, source_target_pairs={{0,0},{2,64},{4,128},{6,192},{64,2},{66,66},{68,130},{70,194},{128... | collective-permute-start | bytes 393224 | tf_op jit(solution)/shard_map/ppermute | solution.py:15
Sparse Core Ops, SparseCore 0:
  9.8 43.7 all-gather.4
  103.5 36.6 all-gather.6
  162.8 43.2 all-gather.8
  210.8 27.6 all-gather.10
  242.5 43.7 reduce-scatter.1

commit v2 on v1

v2 whole, which is shorter than its diff:
```python
import jax
import jax.numpy as jnp
from jax import lax
from jax.experimental import pallas as pl
from jax.experimental.pallas import tpu as pltpu
from jax.sharding import Mesh, PartitionSpec as P

BF = jnp.bfloat16
F32 = jnp.float32
NX, NZ, NY, NC = 4, 8, 4, 2
FEAT = ("y", "c")
CHIPS = ("x", "y")
EXTRA = 16


def swap_xy(v):
    pairs = [(a * NY + b, b * NX + a) for a in range(NX) for b in range(NY)]
    return lax.ppermute(v, ("x", "y"), pairs)


def swap_core(v):
    return lax.ppermute(v, "c", [(0, 1), (1, 0)])


def spread_out(v, axes, n):
    return lax.all_to_all(
        jnp.broadcast_to(v[None], (n,) + v.shape), axes, split_axis=0, concat_axis=0, tiled=True
    )


def split3(v):
    hi = v.astype(BF)
    rest = v - hi.astype(F32)
    mid = rest.astype(BF)
    low = (rest - mid.astype(F32)).astype(BF)
    return hi, mid, low


def dot(a, b, ca, cb):
    return lax.dot_general(a, b, (((ca,), (cb,)), ((), ())), preferred_element_type=F32)


def whole(shape):
    return pl.BlockSpec(shape, lambda j: (0,) * len(shape))


def views_kernel(h_ref, m_ref, w_ref, out_ref):
    ny, nc, nv, rows, kpart = h_ref.shape
    flat = ny * nv * rows
    acc = dot(h_ref[:, 0].reshape(flat, kpart), w_ref[:kpart], 1, 0)
    acc = acc + dot(h_ref[:, 1].reshape(flat, kpart), w_ref[kpart:], 1, 0)
    terms = dot(m_ref[...], w_ref[...], 1, 0)
    mean = terms[0:2] + terms[2:4] + terms[4:6]
    for a in range(ny):
        for v in range(nv):
            lo = (a * nv + v) * rows
            out_ref[0, lo : lo + rows] = (acc[lo : lo + rows] - mean[v : v + 1]).astype(BF)
    hi, mid, low = split3(mean)
    pad = jnp.zeros((EXTRA - 6, mean.shape[1]), F32)
    tail = jnp.concatenate([hi.astype(F32), mid.astype(F32), low.astype(F32), pad], axis=0)
    out_ref[0, flat : flat + EXTRA] = tail.astype(BF)


def weight_kernel(h_ref, g_ref, out_ref):
    ny, nc, nv, rows, kpart = h_ref.shape
    flat = ny * nv * rows
    for c in range(nc):
        out_ref[c * kpart : (c + 1) * kpart] = dot(
            h_ref[:, c].reshape(flat, kpart), g_ref[0], 0, 0
        ).astype(BF)


def input_kernel(g_ref, w_ref, out_ref):
    ny, _, nv, rows, kpart = out_ref.shape
    nx, _, sub = g_ref.shape
    acc = dot(g_ref[0], w_ref[:, :sub], 1, 1)
    for k in range(1, nx):
        acc = acc + dot(g_ref[k], w_ref[:, k * sub : (k + 1) * sub], 1, 1)
    out_ref[:, 0] = acc.astype(BF).reshape(ny, nv, rows, kpart)


def on_device(hidden_first, hidden_second, weight):
    core = lax.axis_index("c")
    first = core == 0
    rows, kpart = hidden_first.shape
    cols = weight.shape[1]
    total_rows = rows * NX * NZ * 1.0
    full_width = cols * NY * NC * 1.0
    blk = rows * NX
    kq = kpart * NC
    sub = cols // NX
    flat = 2 * blk

    wq = lax.all_gather(weight, "z", axis=0, tiled=True)
    moved = swap_xy(jnp.stack([hidden_first, hidden_second]))
    hq = spread_out(moved, FEAT, NY * NC).reshape(NY, NC, 2, rows, kpart)
    row_sum = jnp.sum(hq.astype(F32), axis=(0, 3)).transpose(1, 0, 2).reshape(2, kq)
    mean_in = lax.psum(row_sum, "z") / total_rows
    mean_rows = jnp.concatenate(split3(mean_in) + (jnp.zeros((EXTRA - 6, kq), BF),), axis=0)

    part = pl.pallas_call(
        views_kernel,
        grid=(NX,),
        in_specs=[
            whole(hq.shape),
            whole(mean_rows.shape),
            pl.BlockSpec((kq, sub), lambda j: (0, j)),
        ],
        out_specs=pl.BlockSpec((1, flat + EXTRA, sub), lambda j: (j, 0, 0)),
        out_shape=jax.ShapeDtypeStruct((NX, flat + EXTRA, sub), BF),
        name="views",
    )(hq, mean_rows, wq)
    parts = lax.all_to_all(part, "x", split_axis=0, concat_axis=0, tiled=True)
    summed = jnp.sum(parts.astype(F32), axis=0)
    centered = summed[:flat].reshape(NX, 2, rows, sub).transpose(1, 0, 2, 3).reshape(2, blk, sub)
    mean_cols = summed[flat : flat + 2] + summed[flat + 2 : flat + 4] + summed[flat + 4 : flat + 6]

    half = centered.astype(BF)
    mine = jnp.where(first, half[0], half[1])
    theirs = jnp.where(first, half[1], half[0])
    own_rows = jnp.concatenate([mine, swap_core(theirs)], axis=1)
    gathered = lax.all_gather(own_rows, "z", axis=0, tiled=True)

    variance = lax.psum(jnp.sum(centered * centered, axis=1), "z") / (total_rows - 1.0)
    deviation = jnp.sqrt(variance + 0.0001)
    difference = centered[0] - centered[1] + (mean_cols[0] - mean_cols[1])[None, :]
    share = (
        25.0 * jnp.sum(difference * difference) / (total_rows * full_width)
        + 25.0 * jnp.sum(jax.nn.relu(1.0 - deviation)) / (full_width * NZ)
        - jnp.sum(variance * variance) / (full_width * NZ)
    )
    share = lax.psum(lax.psum(share, "x"), "y")
    gathered, share, difference = lax.optimization_barrier((gathered, share, difference))

    gram_part = dot(own_rows, gathered, 1, 1).astype(BF)
    pieces = lax.all_to_all(
        gram_part.reshape(NX * NY, blk // (NX * NY), -1), CHIPS, split_axis=0, concat_axis=0, tiled=True
    )
    gram_rows = jnp.sum(pieces.astype(F32), axis=0).astype(BF)
    gram_half = spread_out(gram_rows, CHIPS, NX * NY).reshape(blk, -1)
    spread_view = dot(gram_half, gathered, 1, 0)
    spread_own = spread_view[:, :sub]
    spread_back = swap_core(spread_view[:, sub:])
    spread = jnp.stack(
        [jnp.where(first, spread_own, spread_back), jnp.where(first, spread_back, spread_own)]
    )

    inv_grad = 50.0 / 256.0 * jnp.stack([difference, -difference])
    binding = (deviation < 1.0).astype(F32)
    hinge_grad = (
        -(25.0 * total_rows / (256.0 * (total_rows - 1.0)))
        * (binding / deviation)[:, None, :]
        * centered
    )
    cov_grad = (
        4.0
        * total_rows
        / 256.0
        * (spread / (total_rows - 1.0) ** 2 - variance[:, None, :] * centered / (total_rows - 1.0))
    )
    grad_views = (inv_grad + hinge_grad + cov_grad).astype(BF)
    grad_views = grad_views.reshape(2, NX, rows, sub).transpose(1, 0, 2, 3).reshape(flat, sub)
    grads = spread_out(grad_views, "x", NX)

    weight_part = pl.pallas_call(
        weight_kernel,
        grid=(NX,),
        in_specs=[whole(hq.shape), pl.BlockSpec((1, flat, sub), lambda j: (j, 0, 0))],
        out_specs=pl.BlockSpec((kq, sub), lambda j: (0, j)),
        out_shape=jax.ShapeDtypeStruct((kq, cols), BF),
        name="weight_terms",
    )(hq, grads)
    grad_weight = lax.psum_scatter(weight_part, "z", scatter_dimension=0, tiled=True)

    input_part = pl.pallas_call(
        input_kernel,
        grid=(NC,),
        in_specs=[whole(grads.shape), pl.BlockSpec((kpart, cols), lambda j: (j, 0))],
        out_specs=pl.BlockSpec((NY, 1, 2, rows, kpart), lambda j: (0, j, 0, 0, 0)),
        out_shape=jax.ShapeDtypeStruct((NY, NC, 2, rows, kpart), BF),
        name="input_terms",
    )(grads, wq)
    input_parts = lax.all_to_all(
        input_part.reshape(NY * NC, 2, rows, kpart), FEAT, split_axis=0, concat_axis=0, tiled=True
    )
    input_grads = swap_xy(jnp.sum(input_parts.astype(F32), axis=0).astype(BF))

    wide = gram_half.astype(F32)
    share = share + jnp.sum(wide * wide) / ((total_rows - 1.0) ** 2 * full_width)
    share = share.reshape(1, 1)
    total_loss = lax.psum(share + swap_core(share), "z")
    return (total_loss[0, 0], grad_weight, input_grads[0], input_grads[1])


def solution(mesh):
    grid = Mesh(mesh.devices.reshape(NX, NZ, NY, NC), ("x", "z", "y", "c"))
    placed = P(("x", "z"), ("y", "c"))
    return jax.shard_map(
        on_device,
        mesh=grid,
        in_specs=(placed, placed, placed),
        out_specs=(P(), placed, placed, placed),
        check_vma=False,
    )
```

time: 325 us -> 244 us (0.75)
  waiting for transfers between devices: 117 us -> 34.9 us
  Pallas kernels: 0 us -> 13.8 us
  matrix products: 16.2 us -> 3.03 us
  local copies, waits for them, and re-layouts: 14.3 us -> 2.1 us
  starting transfers between devices: 11 us -> 21.3 us
  blocking collectives: 138 us -> 144 us
  other arithmetic: 9.27 us -> 5.79 us
    all_gather x2 -> x0, waiting for transfers between devices: 59.5 us -> none  [the longest x1 31.9 us: on_device(): gram_half = lax.all_gather(gram_rows.astype(BF), CHIPS, axis=0, tiled=True)]
    all_gather x1, waiting for transfers between devices: 36.8 us -> 0.02 us  [on_device(): gathered = lax.all_gather(own_rows, 'z', axis=0, tiled=True)]
    all_to_all x1 -> x3, blocking collectives: 19.2 us -> 54.7 us  [the longest x2 35.1 us: spread_out(): lax.all_to_all(jnp.broadcast_to(v[None], (n,) + v.shape), axes, split_axi...]
    all_gather x2 -> x0, blocking collectives: 31.7 us -> none  [whole_quarter(): got = lax.all_gather(v, FEAT, axis=0, tiled=False)]
    all_to_all x0 -> x1, waiting for transfers between devices: none -> 14.4 us  [spread_out(): lax.all_to_all(jnp.broadcast_to(v[None], (n,) + v.shape), axes, split_axi...]
    pallas_call x0 -> x3, Pallas kernels: none -> 13.8 us  [the longest x1 5.03 us: on_device(): pl.pallas_call(views_kernel, grid=(NX,), in_specs=[whole(hq.shape), whole...]
    dot_general x6 -> x2, matrix products: 16.2 us -> 3.03 us  [dot(): lax.dot_general(a, b, (((ca,), (cb,)), ((), ())), preferred_element_type=...]
    psum x4 -> x5, blocking collectives: 59.9 us -> 70.7 us  [the longest x1 20.3 us: on_device(): mean_in = lax.psum(row_sum, 'z') / total_rows]
  transfers between devices with their start and end apart: 11 -> 10, of which waited for: 7 -> 6; matrix products, arithmetic and copies ran while one was open for 4% -> 3% of each run, Pallas kernels for 0% -> 2%
where the time goes in v2:
time: 244 us; the launch traced here: 243 us
  blocking collectives  144 us (59%)
  waiting for transfers between devices  34.9 us (14%)
  starting transfers between devices  21.3 us (9%)
  between operations  17.9 us (7%)
  Pallas kernels  13.8 us (6%)
  other arithmetic  5.79 us (2%)
  matrix products  3.03 us (1%)
    all_to_all x2, blocking collectives, spread_out(): lax.all_to_all(jnp.broadcast_to(v[None], (n,) + v.shape), axes, split_axi...  35.1 us
    psum x1, blocking collectives, on_device(): mean_in = lax.psum(row_sum, 'z') / total_rows  20.3 us
    all_to_all x1, blocking collectives, on_device(): lax.all_to_all(input_part.reshape(NY * NC, 2, rows, kpart), FEAT, split_a...  19.5 us
    psum x2, blocking collectives, on_device(): share = lax.psum(lax.psum(share, 'x'), 'y')  19 us
    all_to_all x1, blocking collectives, on_device(): lax.all_to_all(gram_part.reshape(NX * NY, blk // (NX * NY), -1), CHIPS, s...  18.7 us
    psum x1, blocking collectives, on_device(): total_loss = lax.psum(share + swap_core(share), 'z')  16.9 us
    psum x1, blocking collectives, on_device(): lax.psum(jnp.sum(centered * centered, axis=1), 'z') / (total_rows - 1.0)  14.5 us
    all_to_all x1, waiting for transfers between devices, spread_out(): lax.all_to_all(jnp.broadcast_to(v[None], (n,) + v.shape), axes, split_axi...  14.4 us
  transfers between devices with their start and end apart: 10, of which 6 were waited for; matrix products, arithmetic and copies ran while one was open for 3% of the time, Pallas kernels for 2%

profile of v2, /device:TPU:8, one launch (start us, length us, event | category | flops | bytes accessed | tf_op | source)
XLA Modules:
  0.0 242.9 jit_solution(5143937506618580820)
XLA Ops:
  8.8 3.3 %collective-permute-start = (bf16[2,64,512]{2,1,0:T(8,128)(2,1)S(1)}, bf16[2,64,512]{2,1,0:T(8,128)(2,1)S(1)}, u32[]{:S(2)}, u32[]{:S(2)}) collective-permute-start(bf16[2,64,512]{2,1,0:T(8,128)(2,1)S(1)} %pad_maximum_fusion.1), channel_id=1, source_target_pairs={{0,0},{2,64},{4,128},{6,192},{64,2},{66,66},{68,130},{70,194},{128... | collective-permute-start | bytes 393224 | tf_op jit(solution)/shard_map/ppermute | solution.py:18
  12.1 4.7 %collective-permute-done = bf16[2,64,512]{2,1,0:T(8,128)(2,1)S(1)} collective-permute-done((bf16[2,64,512]{2,1,0:T(8,128)(2,1)S(1)}, bf16[2,64,512]{2,1,0:T(8,128)(2,1)S(1)}, u32[]{:S(2)}, u32[]{:S(2)}) %collective-permute-start) | collective-permute-done | bytes 131104 | tf_op jit(solution)/shard_map/ppermute | solution.py:18
  16.8 1.1 broadcast_in_dim.10
  17.9 10.0 %all-to-all-start = ((bf16[8,2,64,512]{3,2,1,0:T(8,128)(2,1)}), bf16[8,2,64,512]{3,2,1,0:T(8,128)(2,1)S(1)}, u32[]{:S(2)}, u32[]{:S(2)}) async-start(bf16[8,2,64,512]{3,2,1,0:T(8,128)(2,1)} %broadcast_in_dim.10), calls=%async_computation | async-start | bytes 2097152 | tf_op jit(solution)/shard_map/all_to_all | solution.py:26
  28.0 14.4 %all-to-all-done = bf16[8,2,64,512]{3,2,1,0:T(8,128)(2,1)S(1)} async-done(((bf16[8,2,64,512]{3,2,1,0:T(8,128)(2,1)}), bf16[8,2,64,512]{3,2,1,0:T(8,128)(2,1)S(1)}, u32[]{:S(2)}, u32[]{:S(2)}) %all-to-all-start) | async-done | bytes 1048608 | tf_op jit(solution)/shard_map/all_to_all | solution.py:26
  42.6 20.3 %psum.35 = f32[2,1024]{1,0:T(2,128)S(1)} all-reduce(f32[2,1024]{1,0:T(2,128)S(1)} %bitcast.58), channel_id=1, replica_groups=mesh['x'=4,'z'=8,'y'=4,'c'=2] {'z'}, use_global_device_ids=true, to_apply=%region_2.0 | all-reduce | flops 2048 | bytes 16384 | tf_op jit(solution)/shard_map/psum | solution.py:98
  63.6 5.0 %views.1 = bf16[4,528,256]{2,1,0:T(8,128)(2,1)} custom-call(bf16[4,2,2,64,512]{4,3,2,1,0:T(8,128)(2,1)} %bitcast.40, bf16[16,1024]{1,0:T(8,128)(2,1)} %maximum_maximum_fusion.m_ref, bf16[1024,1024]{1,0:T(8,128)(2,1)} %all-gather.3.cloned.1.call-done.w_ref), custom_call_target="tpu_custom_call" | custom-call | tf_op jit(solution)/shard_map/views/pallas_call | solution.py:101
  68.6 3.6 %all-to-all-start.1 = ((bf16[4,528,256]{2,1,0:T(8,128)(2,1)}), bf16[4,528,256]{2,1,0:T(8,128)(2,1)S(1)}, u32[]{:S(2)}, u32[]{:S(2)}) async-start(bf16[4,528,256]{2,1,0:T(8,128)(2,1)} %views.1), calls=%async_computation.1 | async-start | bytes 2162688 | tf_op jit(solution)/shard_map/all_to_all | solution.py:113
  72.2 11.9 %all-to-all-done.1 = bf16[4,528,256]{2,1,0:T(8,128)(2,1)S(1)} async-done(((bf16[4,528,256]{2,1,0:T(8,128)(2,1)}), bf16[4,528,256]{2,1,0:T(8,128)(2,1)S(1)}, u32[]{:S(2)}, u32[]{:S(2)}) %all-to-all-start.1) | async-done | bytes 1081376 | tf_op jit(solution)/shard_map/all_to_all | solution.py:113
  84.4 1.3 collective-permute-done.1
  88.0 14.5 %psum.36 = f32[2,256]{1,0:T(2,128)S(1)} all-reduce(f32[2,256]{1,0:T(2,128)S(1)} %multiply_reduce_fusion.1), channel_id=1, replica_groups=mesh['x'=4,'z'=8,'y'=4,'c'=2] {'z'}, use_global_device_ids=true, to_apply=%region_6.7 | all-reduce | flops 512 | bytes 4096 | tf_op jit(solution)/shard_map/psum | solution.py:124
  104.4 9.6 %psum.37 = f32[]{:T(128)} all-reduce(f32[]{:T(128)S(6)} %sub.32), channel_id=1, replica_groups=mesh['x'=4,'z'=8,'y'=4,'c'=2] {'x'}, use_global_device_ids=true, to_apply=%region_9.10 | all-reduce | flops 1 | bytes 8 | tf_op jit(solution)/shard_map/psum | solution.py:132
  114.0 9.4 %psum.38 = f32[]{:T(128)} all-reduce(f32[]{:T(128)} %psum.37), channel_id=1, replica_groups=mesh['x'=4,'z'=8,'y'=4,'c'=2] {'y'}, use_global_device_ids=true, to_apply=%region_10.11 | all-reduce | flops 1 | bytes 8 | tf_op jit(solution)/shard_map/psum | solution.py:132
  123.4 2.3 convolution_convert_fusion
  125.8 18.7 %all_to_all.30 = bf16[16,16,2048]{2,1,0:T(8,128)(2,1)S(1)} all-to-all(bf16[16,16,2048]{2,1,0:T(8,128)(2,1)S(1)} %bitcast.45), channel_id=1, replica_groups=mesh['x'=4,'z'=8,'y'=4,'c'=2] {'x','y'}, dimensions={0} | all-to-all | bytes 2097152 | tf_op jit(solution)/shard_map/all_to_all | solution.py:136
  144.8 16.3 %all_to_all.31 = bf16[16,16,2048]{2,1,0:T(8,128)(2,1)S(1)} all-to-all(bf16[16,16,2048]{2,1,0:T(8,128)(2,1)S(1)} %broadcast_in_dim.12), channel_id=1, replica_groups=mesh['x'=4,'z'=8,'y'=4,'c'=2] {'x','y'}, dimensions={0} | all-to-all | bytes 2097152 | tf_op jit(solution)/shard_map/all_to_all | solution.py:26
  162.0 1.5 collective-permute-done.3
  163.8 18.8 %all_to_all.32.g_ref = bf16[4,512,256]{2,1,0:T(8,128)(2,1)} all-to-all(bf16[4,512,256]{2,1,0:T(8,128)(2,1)S(1)} %broadcast_in_dim.14), channel_id=1, replica_groups=mesh['x'=4,'z'=8,'y'=4,'c'=2] {'x'}, dimensions={0} | all-to-all | bytes 2097152 | tf_op jit(solution)/shard_map/all_to_all | solution.py:26
  182.6 4.9 %weight_terms.1 = bf16[1024,1024]{1,0:T(8,128)(2,1)} custom-call(bf16[4,2,2,64,512]{4,3,2,1,0:T(8,128)(2,1)} %bitcast.41, bf16[4,512,256]{2,1,0:T(8,128)(2,1)} %all_to_all.32.g_ref), custom_call_target="tpu_custom_call" | custom-call | tf_op jit(solution)/shard_map/weight_terms/pallas_call | solution.py:165
  187.5 3.9 %input_terms.1 = bf16[4,2,2,64,512]{4,3,2,1,0:T(8,128)(2,1)} custom-call(bf16[4,512,256]{2,1,0:T(8,128)(2,1)} %all_to_all.32.g_ref, bf16[1024,1024]{1,0:T(8,128)(2,1)} %all-gather.3.cloned.1.call-done.w_ref), custom_call_target="tpu_custom_call" | custom-call | tf_op jit(solution)/shard_map/input_terms/pallas_call | solution.py:175
  191.4 19.5 %all_to_all.33 = bf16[8,2,64,512]{3,2,1,0:T(8,128)(2,1)S(1)} all-to-all(bf16[8,2,64,512]{3,2,1,0:T(8,128)(2,1)} %bitcast.46), channel_id=1, replica_groups=mesh['x'=4,'z'=8,'y'=4,'c'=2] {'y','c'}, dimensions={0} | all-to-all | bytes 2097152 | tf_op jit(solution)/shard_map/all_to_all | solution.py:183
  211.1 3.3 %collective-permute-start.4 = (bf16[2,64,512]{2,1,0:T(8,128)(2,1)S(1)}, bf16[2,64,512]{2,1,0:T(8,128)(2,1)S(1)}, u32[]{:S(2)}, u32[]{:S(2)}) collective-permute-start(bf16[2,64,512]{2,1,0:T(8,128)(2,1)S(1)} %reduce_sum.104), channel_id=1, source_target_pairs={{0,0},{2,64},{4,128},{6,192},{64,2},{66,66},{68,130},{70,194},{128... | collective-permute-start | bytes 393224 | tf_op jit(solution)/shard_map/ppermute | solution.py:18
  214.4 1.1 multiply_reduce_fusion
  218.7 16.9 %psum.39 = f32[]{:T(128)} all-reduce(f32[]{:T(128)} %bitcast.15), channel_id=1, replica_groups=mesh['x'=4,'z'=8,'y'=4,'c'=2] {'z'}, use_global_device_ids=true, to_apply=%region_13.14 | all-reduce | flops 1 | bytes 8 | tf_op jit(solution)/shard_map/psum | solution.py:191
  (46 shorter events, 8.6 us)
Async XLA Ops:
  7.2 56.4 %all-gather.3.cloned.1.call-start = ((), (), s32[]{:S(2)}) async-start(), calls=%async_computation.7 | async-start | bytes 2359296 | tf_op jit(solution)/shard_map/all_gather | solution.py:94
  8.8 8.0 %collective-permute-start = (bf16[2,64,512]{2,1,0:T(8,128)(2,1)S(1)}, bf16[2,64,512]{2,1,0:T(8,128)(2,1)S(1)}, u32[]{:S(2)}, u32[]{:S(2)}) collective-permute-start(bf16[2,64,512]{2,1,0:T(8,128)(2,1)S(1)} %pad_maximum_fusion.1), channel_id=1, source_target_pairs={{0,0},{2,64},{4,128},{6,192},{64,2},{66,66},{68,130},{70,194},{128... | collective-permute-start | bytes 393224 | tf_op jit(solution)/shard_map/ppermute | solution.py:18
  17.9 24.4 %all-to-all-start = ((bf16[8,2,64,512]{3,2,1,0:T(8,128)(2,1)}), bf16[8,2,64,512]{3,2,1,0:T(8,128)(2,1)S(1)}, u32[]{:S(2)}, u32[]{:S(2)}) async-start(bf16[8,2,64,512]{3,2,1,0:T(8,128)(2,1)} %broadcast_in_dim.10), calls=%async_computation | async-start | bytes 2097152 | tf_op jit(solution)/shard_map/all_to_all | solution.py:26
  42.3 21.2 %copy-start = (bf16[8,2,64,512]{3,2,1,0:T(8,128)(2,1)}, bf16[8,2,64,512]{3,2,1,0:T(8,128)(2,1)S(1)}, u32[]{:S(2)}) copy-start(bf16[8,2,64,512]{3,2,1,0:T(8,128)(2,1)S(1)} %all-to-all-done) | copy-start | bytes 3145732
  68.6 15.4 %all-to-all-start.1 = ((bf16[4,528,256]{2,1,0:T(8,128)(2,1)}), bf16[4,528,256]{2,1,0:T(8,128)(2,1)S(1)}, u32[]{:S(2)}, u32[]{:S(2)}) async-start(bf16[4,528,256]{2,1,0:T(8,128)(2,1)} %views.1), calls=%async_computation.1 | async-start | bytes 2162688 | tf_op jit(solution)/shard_map/all_to_all | solution.py:113
  72.2 51.3 %all-gather.5.cloned.1.call-start = ((), (), s32[]{:S(2)}) async-start(), calls=%async_computation.8 | async-start | bytes 2359296 | tf_op jit(solution)/shard_map/all_gather | solution.py:122
  84.3 1.4 collective-permute-start.1
  86.5 149.9 %reduce-scatter.2.cloned.1.call-start = ((), (), s32[]{:S(2)}) async-start(), calls=%async_computation.9 | async-start | bytes 2359296 | tf_op jit(solution)/shard_map/reduce_scatter | solution.py:173
  144.7 16.4 %copy-start.1 = (bf16[2048,512]{1,0:T(8,128)(2,1)S(1)}, bf16[2048,512]{1,0:T(8,128)(2,1)}, u32[]{:S(2)}) copy-start(bf16[2048,512]{1,0:T(8,128)(2,1)} %all-gather.5.cloned.1.call-done) | copy-start | bytes 6291460
  161.8 1.6 collective-permute-start.3
  211.1 24.6 %collective-permute-start.4 = (bf16[2,64,512]{2,1,0:T(8,128)(2,1)S(1)}, bf16[2,64,512]{2,1,0:T(8,128)(2,1)S(1)}, u32[]{:S(2)}, u32[]{:S(2)}) collective-permute-start(bf16[2,64,512]{2,1,0:T(8,128)(2,1)S(1)} %reduce_sum.104), channel_id=1, source_target_pairs={{0,0},{2,64},{4,128},{6,192},{64,2},{66,66},{68,130},{70,194},{128... | collective-permute-start | bytes 393224 | tf_op jit(solution)/shard_map/ppermute | solution.py:18
  216.8 1.2 collective-permute-start.2
Sparse Core Ops, SparseCore 0:
  9.8 43.7 all-gather.2
  86.6 36.2 all-gather.4
  187.6 38.2 reduce-scatter.1

commit v3 on v1

v3 whole, which is shorter than its diff:
```python
import jax
import jax.numpy as jnp
from jax import lax
from jax.experimental import pallas as pl
from jax.experimental.pallas import tpu as pltpu
from jax.sharding import Mesh, PartitionSpec as P

BF = jnp.bfloat16
F32 = jnp.float32
NX, NZ, NY, NC = 4, 8, 4, 2
CHIPS = ("x", "y")
SMEM = pltpu.SMEM


def swap_core(v):
    return lax.ppermute(v, "c", [(0, 1), (1, 0)])


def exchange(v, axes):
    return lax.all_to_all(v, axes, split_axis=0, concat_axis=0, tiled=True)


def spread_out(v, axes, n):
    return exchange(jnp.broadcast_to(v[None], (n,) + v.shape), axes)


def split3(v):
    hi = v.astype(BF)
    rest = v - hi.astype(F32)
    mid = rest.astype(BF)
    low = (rest - mid.astype(F32)).astype(BF)
    return hi, mid, low


def dot(a, b, ca, cb):
    return lax.dot_general(a, b, (((ca,), (cb,)), ((), ())), preferred_element_type=F32)


def fixed(shape):
    return pl.BlockSpec(shape, lambda j: (0,) * len(shape))


def at_dim(shape, dim):
    return pl.BlockSpec(shape, lambda j: tuple(j if d == dim else 0 for d in range(len(shape))))


def flat_rows(ref):
    nx, _, nv, rows, width = ref.shape
    return ref[:, 0].reshape(nx * nv * rows, width)


def views_kernel(core_ref, own_ref, oth_ref, m_ref, w_ref, cen_ref, mine_ref, theirs_ref, stat_ref, acc, macc):
    step = pl.program_id(0)
    core = core_ref[0]
    nx, _, nv, rows, _ = own_ref.shape
    w_own = w_ref[0, core]
    w_oth = w_ref[0, 1 - core]
    term = dot(flat_rows(own_ref), w_own, 1, 0) + dot(flat_rows(oth_ref), w_oth, 1, 0)
    mterm = dot(m_ref[0, 0], w_own, 1, 0) + dot(m_ref[0, 1], w_oth, 1, 0)

    @pl.when(step == 0)
    def _():
        acc[...] = term
        macc[...] = mterm

    @pl.when(step > 0)
    def _():
        acc[...] += term
        macc[...] += mterm

    @pl.when(step == pl.num_programs(0) - 1)
    def _():
        terms = macc[...]
        mean = terms[0:2] + terms[2:4] + terms[4:6]
        sums = []
        for v in range(nv):
            total = jnp.zeros((1, mean.shape[1]), F32)
            for a in range(nx):
                lo = (a * nv + v) * rows
                block = acc[lo : lo + rows] - mean[v : v + 1]
                cen_ref[v, a * rows : (a + 1) * rows] = block
                total = total + jnp.sum(block * block, axis=0, keepdims=True)
            sums.append(total)
        stat_ref[...] = jnp.concatenate(sums + [mean, jnp.zeros((4, mean.shape[1]), F32)], axis=0)
        zero = cen_ref[0].astype(BF)
        one = cen_ref[1].astype(BF)
        mine_ref[...] = jnp.where(core == 0, zero, one)
        theirs_ref[...] = jnp.where(core == 0, one, zero)


def weight_kernel(core_ref, own_ref, oth_ref, g_ref, out_ref):
    core = core_ref[0]
    out_ref[0, core] = dot(flat_rows(own_ref), g_ref[...], 0, 0).astype(BF)
    out_ref[0, 1 - core] = dot(flat_rows(oth_ref), g_ref[...], 0, 0).astype(BF)


def input_kernel(core_ref, g_ref, w_ref, out_ref):
    nx, _, nv, rows, width = out_ref.shape
    out_ref[:, 0] = dot(g_ref[...], w_ref[0, core_ref[0]], 1, 1).astype(BF).reshape(nx, nv, rows, width)


def on_device(hidden_first, hidden_second, weight):
    core = lax.axis_index("c")
    core_own = core.astype(jnp.int32).reshape(1)
    first = core == 0
    rows, kpart = hidden_first.shape
    kz, cols = weight.shape
    total_rows = rows * NX * NZ * 1.0
    full_width = cols * NY * NC * 1.0
    blk = rows * NX
    flat = 2 * blk
    sub = cols // NX
    hshape = (NX, NY, 2, rows, kpart)
    hblock = (NX, 1, 2, rows, kpart)
    wblock = (1, NC, kpart, sub)

    w_parts = exchange(jnp.stack([weight[:, k * sub : (k + 1) * sub] for k in range(NX)]), "x")
    moved, w_parts = lax.optimization_barrier((jnp.stack([hidden_first, hidden_second]), w_parts))
    w_all = lax.all_gather(w_parts, "z", axis=1, tiled=True).reshape(NY, NC, kpart, sub)
    h_own = spread_out(moved, CHIPS, NX * NY).reshape(hshape)
    h_oth = swap_core(h_own)

    row_sum = jnp.sum(h_own.astype(F32), axis=(0, 3)).reshape(2 * NY, kpart)
    mean_own = (jnp.sum(spread_out(row_sum, "z", NZ), axis=0) / total_rows).reshape(NY, 2, kpart)
    pad = jnp.zeros((NY, 10, kpart), BF)
    m_own = jnp.concatenate(split3(mean_own) + (pad,), axis=1)
    m_rows = jnp.stack([m_own, swap_core(m_own)], axis=1)

    centered, mine, theirs, stats = pl.pallas_call(
        views_kernel,
        grid=(NY,),
        in_specs=[
            pl.BlockSpec(memory_space=SMEM),
            at_dim(hblock, 1),
            at_dim(hblock, 1),
            at_dim((1, 2, 16, kpart), 0),
            at_dim(wblock, 0),
        ],
        out_specs=[fixed((2, blk, sub)), fixed((blk, sub)), fixed((blk, sub)), fixed((8, sub))],
        out_shape=[
            jax.ShapeDtypeStruct((2, blk, sub), F32),
            jax.ShapeDtypeStruct((blk, sub), BF),
            jax.ShapeDtypeStruct((blk, sub), BF),
            jax.ShapeDtypeStruct((8, sub), F32),
        ],
        scratch_shapes=[pltpu.VMEM((flat, sub), F32), pltpu.VMEM((16, sub), F32)],
        name="views",
    )(core_own, h_own, h_oth, m_rows, w_all)
    mean_cols = stats[2:4]

    own_rows = jnp.concatenate([mine, swap_core(theirs)], axis=1)
    gathered = lax.all_gather(own_rows, "z", axis=0, tiled=True)

    variance = jnp.sum(spread_out(stats, "z", NZ), axis=0)[:2] / (total_rows - 1.0)
    deviation = jnp.sqrt(variance + 0.0001)
    difference = centered[0] - centered[1] + (mean_cols[0] - mean_cols[1])[None, :]
    share = (
        25.0 * jnp.sum(difference * difference) / (total_rows * full_width)
        + 25.0 * jnp.sum(jax.nn.relu(1.0 - deviation)) / (full_width * NZ)
        - jnp.sum(variance * variance) / (full_width * NZ)
    )
    share = jnp.sum(spread_out(jnp.broadcast_to(share, (8, 128)), CHIPS, NX * NY), axis=0)
    gathered, share, difference = lax.optimization_barrier((gathered, share, difference))

    gram_part = dot(own_rows, gathered, 1, 1).astype(BF)
    pieces = exchange(gram_part.reshape(NX * NY, blk // (NX * NY), -1), CHIPS)
    gram_rows = jnp.sum(pieces.astype(F32), axis=0).astype(BF)
    gram_half = spread_out(gram_rows, CHIPS, NX * NY).reshape(blk, -1)
    spread_view = dot(gram_half, gathered, 1, 0)
    spread_own = spread_view[:, :sub]
    spread_back = swap_core(spread_view[:, sub:])
    spread = jnp.stack(
        [jnp.where(first, spread_own, spread_back), jnp.where(first, spread_back, spread_own)]
    )

    inv_grad = 50.0 / 256.0 * jnp.stack([difference, -difference])
    binding = (deviation < 1.0).astype(F32)
    hinge_grad = (
        -(25.0 * total_rows / (256.0 * (total_rows - 1.0)))
        * (binding / deviation)[:, None, :]
        * centered
    )
    cov_grad = (
        4.0
        * total_rows
        / 256.0
        * (spread / (total_rows - 1.0) ** 2 - variance[:, None, :] * centered / (total_rows - 1.0))
    )
    grad_views = (inv_grad + hinge_grad + cov_grad).astype(BF)
    grads = grad_views.reshape(2, NX, rows, sub).transpose(1, 0, 2, 3).reshape(flat, sub)

    weight_part = pl.pallas_call(
        weight_kernel,
        grid=(NY,),
        in_specs=[
            pl.BlockSpec(memory_space=SMEM),
            at_dim(hblock, 1),
            at_dim(hblock, 1),
            fixed((flat, sub)),
        ],
        out_specs=at_dim(wblock, 0),
        out_shape=jax.ShapeDtypeStruct((NY, NC, kpart, sub), BF),
        name="weight_terms",
    )(core_own, h_own, h_oth, grads)
    weight_sum = lax.psum_scatter(
        weight_part.reshape(NX, NZ * kz, sub), "z", scatter_dimension=1, tiled=True
    )

    def input_terms(which):
        return pl.pallas_call(
            input_kernel,
            grid=(NY,),
            in_specs=[pl.BlockSpec(memory_space=SMEM), fixed((flat, sub)), at_dim(wblock, 0)],
            out_specs=at_dim(hblock, 1),
            out_shape=jax.ShapeDtypeStruct(hshape, BF),
            name="input_terms",
        )(which, grads, w_all)

    from_other = swap_core(input_terms(1 - core_own))
    input_sum = (input_terms(core_own).astype(F32) + from_other.astype(F32)).astype(BF)
    input_parts = exchange(input_sum.reshape(NX * NY, 2, rows, kpart), CHIPS)
    input_grads = jnp.sum(input_parts.astype(F32), axis=0).astype(BF)

    wide = gram_half.astype(F32)
    share = share + jnp.sum(wide * wide) / ((total_rows - 1.0) ** 2 * full_width)
    total_loss = jnp.sum(spread_out(share, ("z", "c"), NZ * NC), axis=0)[0, 0]

    blocks = exchange(weight_sum, "x")
    grad_weight = jnp.concatenate([blocks[k] for k in range(NX)], axis=1)
    return (total_loss, grad_weight, input_grads[0], input_grads[1])


def solution(mesh):
    grid = Mesh(mesh.devices.reshape(NX, NZ, NY, NC), ("x", "z", "y", "c"))
    placed = P(("x", "z"), ("y", "c"))
    return jax.shard_map(
        on_device,
        mesh=grid,
        in_specs=(placed, placed, placed),
        out_specs=(P(), placed, placed, placed),
        check_vma=False,
    )
```

time: 325 us -> 245 us (0.75)
  blocking collectives: 138 us -> 49.1 us
  starting transfers between devices: 11 us -> 35.5 us
  waiting for transfers between devices: 117 us -> 97 us
  Pallas kernels: 0 us -> 19.8 us
  matrix products: 16.2 us -> 3.13 us
  local copies, waits for them, and re-layouts: 14.3 us -> 9.11 us
    all_to_all x1 -> x7, waiting for transfers between devices: 12 us -> 82.9 us  [exchange(): return lax.all_to_all(v, axes, split_axis=0, concat_axis=0, tiled=True)]
    psum x4 -> x0, blocking collectives: 59.9 us -> none  [the longest x3 39.6 us: on_device(): total_loss = lax.psum(lax.psum(lax.psum(share, 'x'), FEAT), 'z')]
    all_gather x3 -> x1, waiting for transfers between devices: 59.5 us -> 0.01 us  [on_device(): lax.all_gather(w_parts, 'z', axis=1, tiled=True).reshape(NY, NC, kpart, sub)]
    all_gather x2 -> x0, blocking collectives: 31.7 us -> none  [whole_quarter(): got = lax.all_gather(v, FEAT, axis=0, tiled=False)]
    all_to_all x1 -> x7, starting transfers between devices: 3.51 us -> 34.9 us  [exchange(): return lax.all_to_all(v, axes, split_axis=0, concat_axis=0, tiled=True)]
    all_gather x1, waiting for transfers between devices: 36.8 us -> 10.1 us  [on_device(): gathered = lax.all_gather(own_rows, 'z', axis=0, tiled=True)]
    pallas_call x0 -> x4, Pallas kernels: none -> 19.8 us  [the longest x2 9.02 us: input_terms(): pl.pallas_call(input_kernel, grid=(NY,), in_specs=[pl.BlockSpec(memory_sp...]
    dot_general x6 -> x2, matrix products: 16.2 us -> 3.13 us  [dot(): lax.dot_general(a, b, (((ca,), (cb,)), ((), ())), preferred_element_type=...]
  transfers between devices with their start and end apart: 11 -> 15, of which waited for: 7 -> 11; matrix products, arithmetic and copies ran while one was open for 4% -> 6% of each run, Pallas kernels for 0% -> 4%
where the time goes in v3:
time: 245 us; the launch traced here: 242 us
  waiting for transfers between devices  97 us (40%)
  blocking collectives  49.1 us (20%)
  starting transfers between devices  35.5 us (14%)
  Pallas kernels  19.8 us (8%)
  between operations  16.6 us (7%)
  other arithmetic  12.2 us (5%)
  local copies, waits for them, and re-layouts  9.11 us (4%)
  matrix products  3.13 us (1%)
    all_to_all x7, waiting for transfers between devices, exchange(): return lax.all_to_all(v, axes, split_axis=0, concat_axis=0, tiled=True)  82.9 us
    all_to_all x3, blocking collectives, exchange(): return lax.all_to_all(v, axes, split_axis=0, concat_axis=0, tiled=True)  49.1 us
    all_to_all x7, starting transfers between devices, exchange(): return lax.all_to_all(v, axes, split_axis=0, concat_axis=0, tiled=True)  34.9 us
    all_gather x1, waiting for transfers between devices, on_device(): gathered = lax.all_gather(own_rows, 'z', axis=0, tiled=True)  10.1 us
    pallas_call x2, Pallas kernels, input_terms(): pl.pallas_call(input_kernel, grid=(NY,), in_specs=[pl.BlockSpec(memory_sp...  9.02 us
    pallas_call x1, Pallas kernels, on_device(): pl.pallas_call(views_kernel, grid=(NY,), in_specs=[pl.BlockSpec(memory_sp...  5.6 us
    pallas_call x1, Pallas kernels, on_device(): pl.pallas_call(weight_kernel, grid=(NY,), in_specs=[pl.BlockSpec(memory_s...  5.14 us
  transfers between devices with their start and end apart: 15, of which 11 were waited for; matrix products, arithmetic and copies ran while one was open for 6% of the time, Pallas kernels for 4%

profile of v3, /device:TPU:8, one launch (start us, length us, event | category | flops | bytes accessed | tf_op | source)
XLA Modules:
  0.0 242.4 jit_solution(9156399040543666831)
XLA Ops:
  8.9 4.3 %all-to-all-start = ((bf16[4,128,256]{2,1,0:T(8,128)(2,1)}), bf16[4,128,256]{2,1,0:T(8,128)(2,1)S(1)}, u32[]{:S(2)}, u32[]{:S(2)}) async-start(bf16[4,128,256]{2,1,0:T(8,128)(2,1)} %pad_maximum_fusion), calls=%async_computation | async-start | bytes 524288 | tf_op jit(solution)/shard_map/all_to_all | solution.py:20
  14.0 5.8 %all-to-all-done = bf16[4,128,256]{2,1,0:T(8,128)(2,1)S(1)} async-done(((bf16[4,128,256]{2,1,0:T(8,128)(2,1)}), bf16[4,128,256]{2,1,0:T(8,128)(2,1)S(1)}, u32[]{:S(2)}, u32[]{:S(2)}) %all-to-all-start) | async-done | bytes 262176 | tf_op jit(solution)/shard_map/all_to_all | solution.py:20
  21.4 5.5 %all-to-all-start.1 = ((bf16[16,2,64,512]{3,2,1,0:T(8,128)(2,1)}), bf16[16,2,64,512]{3,2,1,0:T(8,128)(2,1)S(1)}, u32[]{:S(2)}, u32[]{:S(2)}) async-start(bf16[16,2,64,512]{3,2,1,0:T(8,128)(2,1)} %broadcast_in_dim.14), calls=%async_computation.1 | async-start | bytes 4194304 | tf_op jit(solution)/shard_map/all_to_all | solution.py:20
  27.7 26.2 %all-to-all-done.1 = bf16[16,2,64,512]{3,2,1,0:T(8,128)(2,1)S(1)} async-done(((bf16[16,2,64,512]{3,2,1,0:T(8,128)(2,1)}), bf16[16,2,64,512]{3,2,1,0:T(8,128)(2,1)S(1)}, u32[]{:S(2)}, u32[]{:S(2)}) %all-to-all-start.1) | async-done | bytes 2097184 | tf_op jit(solution)/shard_map/all_to_all | solution.py:20
  55.2 8.5 %all-to-all-start.2 = ((f32[8,8,512]{2,1,0:T(8,128)}), f32[8,8,512]{2,1,0:T(8,128)S(1)}, u32[]{:S(2)}, u32[]{:S(2)}) async-start(f32[8,8,512]{2,1,0:T(8,128)} %broadcast_in_dim.16), calls=%async_computation.2 | async-start | bytes 262144 | tf_op jit(solution)/shard_map/all_to_all | solution.py:20
  63.8 10.2 %all-to-all-done.2 = f32[8,8,512]{2,1,0:T(8,128)S(1)} async-done(((f32[8,8,512]{2,1,0:T(8,128)}), f32[8,8,512]{2,1,0:T(8,128)S(1)}, u32[]{:S(2)}, u32[]{:S(2)}) %all-to-all-start.2) | async-done | bytes 131104 | tf_op jit(solution)/shard_map/all_to_all | solution.py:20
  76.2 5.6 %views.1 = (f32[2,256,256]{2,1,0:T(8,128)}, bf16[256,256]{1,0:T(8,128)(2,1)}, bf16[256,256]{1,0:T(8,128)(2,1)}, f32[8,256]{1,0:T(8,128)}) custom-call(s32[1]{0:T(128)} %bitcast.core_ref, bf16[4,4,2,64,512]{4,3,2,1,0:T(8,128)(2,1)} %bitcast.56, bf16[4,4,2,64,512]{4,3,2,1,0:T(8,128)(2,1)} %collective-permute-done.oth_ref, ...), custom_call_target="tpu_custom_call" | custom-call | tf_op jit(solution)/shard_map/views/pallas_call | solution.py:129
  85.4 3.8 %all-to-all-start.3 = ((f32[8,8,256]{2,1,0:T(8,128)}), f32[8,8,256]{2,1,0:T(8,128)S(1)}, u32[]{:S(2)}, u32[]{:S(2)}) async-start(f32[8,8,256]{2,1,0:T(8,128)} %broadcast_in_dim.18), calls=%async_computation.3 | async-start | bytes 131072 | tf_op jit(solution)/shard_map/all_to_all | solution.py:20
  90.0 1.7 multiply_reduce_fusion.1
  92.4 5.2 %all-to-all-done.3 = f32[8,8,256]{2,1,0:T(8,128)S(1)} async-done(((f32[8,8,256]{2,1,0:T(8,128)}), f32[8,8,256]{2,1,0:T(8,128)S(1)}, u32[]{:S(2)}, u32[]{:S(2)}) %all-to-all-start.3) | async-done | bytes 65568 | tf_op jit(solution)/shard_map/all_to_all | solution.py:20
  99.5 14.0 %all_to_all.50 = f32[16,8,128]{2,1,0:T(8,128)S(1)} all-to-all(f32[16,8,128]{2,1,0:T(8,128)S(1)} %broadcast_in_dim_broadcast_in_dim_broadcast_in_dim.3), channel_id=1, replica_groups=mesh['x'=4,'z'=8,'y'=4,'c'=2] {'x','y'}, dimensions={0} | all-to-all | bytes 131072 | tf_op jit(solution)/shard_map/all_to_all | solution.py:20
  113.6 10.1 %all-gather.5.cloned.1.call-done = bf16[2048,512]{1,0:T(8,128)(2,1)} async-done(((bf16[256,512]{1,0:T(8,128)(2,1)}), bf16[2048,512]{1,0:T(8,128)(2,1)}) %all-gather.5.cloned.1.call-update) | async-done | bytes 2097168 | tf_op jit(solution)/shard_map/all_gather | solution.py:152
  123.7 2.4 %convolution_convert_fusion = bf16[256,2048]{1,0:T(8,128)(2,1)S(1)} fusion(bf16[256,512]{1,0:T(8,128)(2,1)} %copy-done.3, bf16[2048,512]{1,0:T(8,128)(2,1)} %all-gather.5.cloned.1.call-done), kind=kOutput, calls=%fused_computation.2 | convolution fusion | flops 537395200 | bytes 3407872 | tf_op jit(solution)/shard_map/dot_general | solution.py:36
  126.1 18.8 %all_to_all.51 = bf16[16,16,2048]{2,1,0:T(8,128)(2,1)S(1)} all-to-all(bf16[16,16,2048]{2,1,0:T(8,128)(2,1)S(1)} %bitcast.63), channel_id=1, replica_groups=mesh['x'=4,'z'=8,'y'=4,'c'=2] {'x','y'}, dimensions={0} | all-to-all | bytes 2097152 | tf_op jit(solution)/shard_map/all_to_all | solution.py:20
  145.2 16.3 %all_to_all.52 = bf16[16,16,2048]{2,1,0:T(8,128)(2,1)S(1)} all-to-all(bf16[16,16,2048]{2,1,0:T(8,128)(2,1)S(1)} %broadcast_in_dim.19), channel_id=1, replica_groups=mesh['x'=4,'z'=8,'y'=4,'c'=2] {'x','y'}, dimensions={0} | all-to-all | bytes 2097152 | tf_op jit(solution)/shard_map/all_to_all | solution.py:20
  164.8 4.4 %input_terms.3 = bf16[4,4,2,64,512]{4,3,2,1,0:T(8,128)(2,1)} custom-call(s32[1]{0:T(128)S(6)} %sub.36.core_ref, bf16[512,256]{1,0:T(8,128)(2,1)} %bitcast.64, bf16[4,2,512,256]{3,2,1,0:T(8,128)(2,1)} %bitcast.59), custom_call_target="tpu_custom_call" | custom-call | tf_op jit(solution)/shard_map/input_terms/pallas_call | solution.py:210
  169.4 5.1 %weight_terms.1 = bf16[4,2,512,256]{3,2,1,0:T(8,128)(2,1)} custom-call(s32[1]{0:T(128)} %bitcast.core_ref, bf16[4,4,2,64,512]{4,3,2,1,0:T(8,128)(2,1)} %bitcast.57, bf16[4,4,2,64,512]{4,3,2,1,0:T(8,128)(2,1)} %collective-permute-done.oth_ref, bf16[512,256]{1,0:T(8,128)(2,1)} %bitcast.65), custom_call_target="tpu_custom_call" | custom-call | tf_op jit(solution)/shard_map/weight_terms/pallas_call | solution.py:192
  177.0 4.3 %all-to-all-start.7 = ((f32[16,8,128]{2,1,0:T(8,128)}), f32[16,8,128]{2,1,0:T(8,128)S(1)}, u32[]{:S(2)}, u32[]{:S(2)}) async-start(f32[16,8,128]{2,1,0:T(8,128)} %broadcast_in_dim.20), calls=%async_computation.7 | async-start | bytes 131072 | tf_op jit(solution)/shard_map/all_to_all | solution.py:20
  181.3 4.6 %input_terms.2 = bf16[4,4,2,64,512]{4,3,2,1,0:T(8,128)(2,1)} custom-call(s32[1]{0:T(128)} %bitcast.core_ref, bf16[512,256]{1,0:T(8,128)(2,1)} %bitcast.66, bf16[4,2,512,256]{3,2,1,0:T(8,128)(2,1)} %bitcast.60), custom_call_target="tpu_custom_call" | custom-call | tf_op jit(solution)/shard_map/input_terms/pallas_call | solution.py:210
  185.9 3.6 %add_convert_fusion = bf16[4,4,2,64,512]{4,3,2,1,0:T(8,128)(2,1)} fusion(bf16[4,4,2,64,512]{4,3,2,1,0:T(8,128)(2,1)S(1)} %collective-permute-done.4, bf16[4,4,2,64,512]{4,3,2,1,0:T(8,128)(2,1)} %input_terms.2), kind=kLoop, calls=%fused_computation | loop fusion | flops 4194304 | bytes 6291456 | tf_op jit(solution)/shard_map/convert_element_type | solution.py:220
  189.8 4.9 %all-to-all-start.9 = ((bf16[16,2,64,512]{3,2,1,0:T(8,128)(2,1)}), bf16[16,2,64,512]{3,2,1,0:T(8,128)(2,1)S(1)}, u32[]{:S(2)}, u32[]{:S(2)}) async-start(bf16[16,2,64,512]{3,2,1,0:T(8,128)(2,1)} %bitcast.31), calls=%async_computation.10 | async-start | bytes 4194304 | tf_op jit(solution)/shard_map/all_to_all | solution.py:20
  195.2 29.2 %all-to-all-done.9 = bf16[16,2,64,512]{3,2,1,0:T(8,128)(2,1)S(1)} async-done(((bf16[16,2,64,512]{3,2,1,0:T(8,128)(2,1)}), bf16[16,2,64,512]{3,2,1,0:T(8,128)(2,1)S(1)}, u32[]{:S(2)}, u32[]{:S(2)}) %all-to-all-start.9) | async-done | bytes 2097184 | tf_op jit(solution)/shard_map/all_to_all | solution.py:20
  224.7 3.7 %all-to-all-start.8 = ((bf16[4,128,256]{2,1,0:T(8,128)(2,1)}), bf16[4,128,256]{2,1,0:T(8,128)(2,1)S(1)}, u32[]{:S(2)}, u32[]{:S(2)}) async-start(bf16[4,128,256]{2,1,0:T(8,128)(2,1)} %reduce-scatter.2.cloned.1.call-done), calls=%async_computation.9 | async-start | bytes 524288 | tf_op jit(solution)/shard_map/all_to_all | solution.py:20
  229.1 6.0 %all-to-all-done.8 = bf16[4,128,256]{2,1,0:T(8,128)(2,1)S(1)} async-done(((bf16[4,128,256]{2,1,0:T(8,128)(2,1)}), bf16[4,128,256]{2,1,0:T(8,128)(2,1)S(1)}, u32[]{:S(2)}, u32[]{:S(2)}) %all-to-all-start.8) | async-done | bytes 262176 | tf_op jit(solution)/shard_map/all_to_all | solution.py:20
  (70 shorter events, 21.6 us)
Async XLA Ops:
  8.9 11.0 %all-to-all-start = ((bf16[4,128,256]{2,1,0:T(8,128)(2,1)}), bf16[4,128,256]{2,1,0:T(8,128)(2,1)S(1)}, u32[]{:S(2)}, u32[]{:S(2)}) async-start(bf16[4,128,256]{2,1,0:T(8,128)(2,1)} %pad_maximum_fusion), calls=%async_computation | async-start | bytes 524288 | tf_op jit(solution)/shard_map/all_to_all | solution.py:20
  19.8 1.6 copy-start.4
  21.4 32.5 %all-to-all-start.1 = ((bf16[16,2,64,512]{3,2,1,0:T(8,128)(2,1)}), bf16[16,2,64,512]{3,2,1,0:T(8,128)(2,1)S(1)}, u32[]{:S(2)}, u32[]{:S(2)}) async-start(bf16[16,2,64,512]{3,2,1,0:T(8,128)(2,1)} %broadcast_in_dim.14), calls=%async_computation.1 | async-start | bytes 4194304 | tf_op jit(solution)/shard_map/all_to_all | solution.py:20
  26.9 49.2 %all-gather.3.cloned.1.call-start = ((), (), s32[]{:S(2)}) async-start(), calls=%async_computation.11 | async-start | bytes 2359296 | tf_op jit(solution)/shard_map/all_gather | solution.py:119
  53.9 22.3 %copy-start = (bf16[16,2,64,512]{3,2,1,0:T(8,128)(2,1)}, bf16[16,2,64,512]{3,2,1,0:T(8,128)(2,1)S(1)}, u32[]{:S(2)}) copy-start(bf16[16,2,64,512]{3,2,1,0:T(8,128)(2,1)S(1)} %all-to-all-done.1) | copy-start | bytes 6291460
  53.9 22.3 %collective-permute-start = (bf16[4,4,2,64,512]{4,3,2,1,0:T(8,128)(2,1)S(1)}, bf16[4,4,2,64,512]{4,3,2,1,0:T(8,128)(2,1)}, u32[]{:S(2)}, u32[]{:S(2)}) collective-permute-start(bf16[4,4,2,64,512]{4,3,2,1,0:T(8,128)(2,1)S(1)} %bitcast.55), channel_id=1, source_target_pairs={{0,1},{1,0},{2,3},{3,2},{4,5},{5,4},{6,7},{7,6},{8,9},{9,8},{10,11... | collective-permute-start | bytes 6291464 | tf_op jit(solution)/shard_map/ppermute | solution.py:16
  55.2 18.7 %all-to-all-start.2 = ((f32[8,8,512]{2,1,0:T(8,128)}), f32[8,8,512]{2,1,0:T(8,128)S(1)}, u32[]{:S(2)}, u32[]{:S(2)}) async-start(f32[8,8,512]{2,1,0:T(8,128)} %broadcast_in_dim.16), calls=%async_computation.2 | async-start | bytes 262144 | tf_op jit(solution)/shard_map/all_to_all | solution.py:20
  63.7 60.0 %all-gather.5.cloned.1.call-start = ((), (), s32[]{:S(2)}) async-start(), calls=%async_computation.12 | async-start | bytes 2359296 | tf_op jit(solution)/shard_map/all_gather | solution.py:152
  74.2 1.3 collective-permute-start.1
  81.8 1.6 collective-permute-start.2
  83.3 0.7 copy-start.3
  85.4 12.2 %all-to-all-start.3 = ((f32[8,8,256]{2,1,0:T(8,128)}), f32[8,8,256]{2,1,0:T(8,128)S(1)}, u32[]{:S(2)}, u32[]{:S(2)}) async-start(f32[8,8,256]{2,1,0:T(8,128)} %broadcast_in_dim.18), calls=%async_computation.3 | async-start | bytes 131072 | tf_op jit(solution)/shard_map/all_to_all | solution.py:20
  89.2 135.5 %reduce-scatter.2.cloned.1.call-start = ((), (), s32[]{:S(2)}) async-start(), calls=%async_computation.13 | async-start | bytes 2359296 | tf_op jit(solution)/shard_map/reduce_scatter | solution.py:205
  145.1 16.4 %copy-start.2 = (bf16[2048,512]{1,0:T(8,128)(2,1)S(1)}, bf16[2048,512]{1,0:T(8,128)(2,1)}, u32[]{:S(2)}) copy-start(bf16[2048,512]{1,0:T(8,128)(2,1)} %all-gather.5.cloned.1.call-done) | copy-start | bytes 6291460
  161.5 2.4 copy-start.1
  162.2 1.6 collective-permute-start.3
  169.2 16.6 %collective-permute-start.4 = (bf16[4,4,2,64,512]{4,3,2,1,0:T(8,128)(2,1)}, bf16[4,4,2,64,512]{4,3,2,1,0:T(8,128)(2,1)S(1)}, u32[]{:S(2)}, u32[]{:S(2)}) collective-permute-start(bf16[4,4,2,64,512]{4,3,2,1,0:T(8,128)(2,1)} %input_terms.3), channel_id=1, source_target_pairs={{0,1},{1,0},{2,3},{3,2},{4,5},{5,4},{6,7},{7,6},{8,9},{9,8},{10,11... | collective-permute-start | bytes 6291464 | tf_op jit(solution)/shard_map/ppermute | solution.py:16
  177.0 12.9 %all-to-all-start.7 = ((f32[16,8,128]{2,1,0:T(8,128)}), f32[16,8,128]{2,1,0:T(8,128)S(1)}, u32[]{:S(2)}, u32[]{:S(2)}) async-start(f32[16,8,128]{2,1,0:T(8,128)} %broadcast_in_dim.20), calls=%async_computation.7 | async-start | bytes 131072 | tf_op jit(solution)/shard_map/all_to_all | solution.py:20
  189.8 34.6 %all-to-all-start.9 = ((bf16[16,2,64,512]{3,2,1,0:T(8,128)(2,1)}), bf16[16,2,64,512]{3,2,1,0:T(8,128)(2,1)S(1)}, u32[]{:S(2)}, u32[]{:S(2)}) async-start(bf16[16,2,64,512]{3,2,1,0:T(8,128)(2,1)} %bitcast.31), calls=%async_computation.10 | async-start | bytes 4194304 | tf_op jit(solution)/shard_map/all_to_all | solution.py:20
  224.7 10.4 %all-to-all-start.8 = ((bf16[4,128,256]{2,1,0:T(8,128)(2,1)}), bf16[4,128,256]{2,1,0:T(8,128)(2,1)S(1)}, u32[]{:S(2)}, u32[]{:S(2)}) async-start(bf16[4,128,256]{2,1,0:T(8,128)(2,1)} %reduce-scatter.2.cloned.1.call-done), calls=%async_computation.9 | async-start | bytes 524288 | tf_op jit(solution)/shard_map/all_to_all | solution.py:20
Sparse Core Ops, SparseCore 0:
  30.1 44.8 all-gather.2
  84.2 39.4 all-gather.4
  174.7 39.7 reduce-scatter.1
